TPU v7x, 32 devices: a whole 2x2x4 slice. The times are simulated.
32 devices in a mesh: row: 8 (over z, y), col: 4 (over x, core).
Axes of the slice: x: 2, y: 2, z: 4, core: 2. Of those that a mesh axis runs over, the one named last changes fastest.
Arguments:
- three_index: bfloat16 [8, 4, 8, 2, 128, 128], P('row', 'col'), may hold values from -6 to 6
- slot_pair: int32 [8, 4, 8], P('row', 'col'), may hold values from -1 to 31, as said below
- coeff: bfloat16 [4096, 256], P(('col', 'row')), may hold values from -0.125 to 0.125
- occ_mask: int32 [32, 2], P('col'), may hold values 0 or 1
Outputs:
- exchange_block: bfloat16 [4096, 4096], P('row', 'col')
Inputs may be any that keep to these rules, and one draw needn't show every extreme that they name: `slot_pair`: on each device (first two dimensions) the 8 slots name distinct local pair blocks mb * 8 + nb, the live ones first and -1 after them; in every draw some device fills all 8 slots.
All inputs are finite; a program needn't handle non-finite values. No bound on the sum of `occ_mask` on one device may be relied on, other than what follows from the above.
Results may differ from a plain program's by a relative error of at most 0.0057.
Values may be sent and summed in bfloat16 or wider, within the bound.
No kernel may reach another device: no remote copies, remote signals or barrier semaphores. Data moves between devices by JAX's collectives and lax.ppermute only.
A program may use at most 64 MiB of HBM per device.

v0:
```python
import jax
import jax.numpy as jnp
from jax import lax
from jax.sharding import PartitionSpec as P

MB_DEV = 4


def spread(value, axis, root):
    mine = lax.axis_index(axis) == root
    return lax.psum(jnp.where(mine, value, jnp.zeros_like(value)), axis)


def body(three_index, slot_pair, coeff, occ_mask):
    block_size = three_index.shape[4]
    aux_count = three_index.shape[3]
    occ_count = coeff.shape[1]
    gathered = lax.all_gather(coeff, "row", axis=0, tiled=True)
    nu_blocks = gathered.shape[0] // block_size
    occ_blocks = occ_count // block_size
    keep = occ_mask.astype(jnp.bfloat16)[:, None, :, None]
    masked = (gathered.reshape(nu_blocks, block_size, occ_blocks, block_size) * keep).reshape(
        gathered.shape[0], occ_count
    )
    blocks = three_index[0, 0]
    slots = slot_pair[0, 0]
    mu_rows_count = MB_DEV * block_size
    live_count = jnp.sum((slots >= 0).astype(jnp.int32))

    def add_slot(slot_index, partial_value):
        pair = slots[slot_index]
        mu_start = pair // nu_blocks * block_size
        nu_start = pair % nu_blocks * block_size
        rows = lax.dynamic_slice_in_dim(masked, nu_start, block_size, 0)
        term = jnp.einsum(
            "pab,bi->api", blocks[slot_index], rows, preferred_element_type=jnp.float32
        )
        current = lax.dynamic_slice_in_dim(partial_value, mu_start, block_size, 0)
        return lax.dynamic_update_slice_in_dim(partial_value, current + term, mu_start, 0)

    partial_value = jnp.zeros((mu_rows_count, aux_count, occ_count), jnp.float32)
    partial_value = lax.fori_loop(0, live_count, add_slot, partial_value)
    ratio = lax.axis_size("row") // lax.axis_size("col")
    col_place = lax.axis_index("col")
    mu_half = lax.psum(partial_value, "col").astype(jnp.bfloat16)
    pieces = []
    for mirror in range(ratio):
        pieces.append(spread(mu_half, "row", ratio * col_place + mirror))
    nu_half = jnp.concatenate(pieces, 0)
    left = mu_half.reshape(mu_rows_count, aux_count * occ_count)
    right = nu_half.reshape(nu_half.shape[0], aux_count * occ_count)
    product = lax.dot_general(
        left, right, (((1,), (1,)), ((), ())), preferred_element_type=jnp.float32
    )
    return (product / jnp.sqrt(jnp.float32(aux_count * occ_count))).astype(jnp.bfloat16)


def solution(mesh):
    return jax.shard_map(
        body,
        mesh=mesh,
        in_specs=(
            P("row", "col", None, None, None, None),
            P("row", "col", None),
            P(("col", "row"), None),
            P("col", None),
        ),
        out_specs=P("row", "col"),
        check_vma=False,
    )
```

profile of v0, /device:TPU:0, one launch (start us, length us, event | category | flops | bytes accessed | tf_op | source)
XLA Modules:
  0.0 192.0 jit_solution(16867687880733982412)
XLA Ops:
  6.5 0.0 all-reduce.4.cloned.1.call-start
  6.5 1.4 fusion.10
  7.9 0.7 convert_element_type.13
  8.6 0.9 copy.5
  9.5 29.6 %all_gather.3 = bf16[1024,256]{0,1:T(8,128)(2,1)S(1)} all-gather(bf16[128,256]{0,1:T(8,128)(2,1)S(1)} %copy.5), channel_id=1, replica_groups=mesh['row'=8,'col'=4] {'row'}, dimensions={0}, use_global_device_ids=true | all-gather | bytes 589824 | tf_op jit(solution)/shard_map/all_gather | solution.py:18
  39.1 0.1 mul.27
  39.2 0.0 copy-start
  39.2 0.1 bitcast_multiply_fusion.1
  39.3 0.1 broadcast_in_dim.4.clone
  39.4 0.5 copy-done
  39.9 15.5 %while.12 = (s32[]{:T(128)}, f32[512,2,256]{2,0,1:T(8,128)S(1)}, s32[]{:T(128)}, s32[8]{0:T(128)S(1)}, bf16[1024,256]{0,1:T(8,128)(2,1)S(1)}, /*index=5*/bf16[8,...) while((s32[]{:T(128)}, f32[512,2,256]{2,0,1:T(8,128)S(1)}, ...), condition=%wide.region_2.3_spmd, body=%wide.region_1.2_spmd.sunk | while | flops 16842784 | bytes 2753002 | solution.py:42
  40.6 0.6 dynamic_slice.40
  43.5 0.1 copy.14
  43.6 1.0 fusion.19
  44.6 0.1 copy.15
  45.5 0.6 dynamic_slice.40
  48.4 0.1 copy.14
  48.5 1.0 fusion.19
  49.6 0.1 copy.15
  50.5 0.6 dynamic_slice.40
  53.3 0.1 copy.14
  53.5 1.0 fusion.19
  54.5 0.1 copy.15
  55.4 50.0 %all-reduce.5 = bf16[512,2,256]{2,0,1:T(8,128)(2,1)S(1)} all-reduce(f32[512,2,256]{2,0,1:T(8,128)S(1)} %get-tuple-element.88), channel_id=1, replica_groups=mesh['row'=8,'col'=4] {'col'}, use_global_device_ids=true, to_apply=%region_3.4 | all-reduce | flops 262144 | bytes 1572864 | tf_op jit(solution)/shard_map/psum | solution.py:45
  105.4 1.1 broadcast_select_fusion.1
  106.5 0.0 all-reduce.4.cloned.1.call-update
  106.5 75.7 %all-reduce.4.cloned.1.call-done = (bf16[512,2,256]{2,0,1:T(8,128)(2,1)}, bf16[512,2,256]{2,0,1:T(8,128)(2,1)}) async-done(((bf16[512,2,256]{2,0,1:T(8,128)(2,1)}, bf16[512,2,256]{2,0,1:T(8,128)(2,1)}), (bf16[512,2,256]{2,0,1:T(8,128)(2,1)}, bf16[512,2,256]{2,0,1:T(8,128)(2,1)})) %all-reduce.4.cloned.1.call-update) | async-done | bytes 1048592 | tf_op jit(solution)/shard_map/psum | solution.py:11
  182.3 2.9 %fusion.6 = bf16[512,1024]{1,0:T(8,128)(2,1)} fusion(bf16[512,2,256]{2,0,1:T(8,128)(2,1)} %get-tuple-element.101, bf16[512,2,256]{2,0,1:T(8,128)(2,1)} %get-tuple-element.102, bf16[512,2,256]{2,0,1:T(8,128)(2,1)S(1)} %all-reduce.5), kind=kOutput, calls=%fused_computation.10 | convolution fusion | flops 540016640 | bytes 2621440 | tf_op jit(solution)/shard_map/dot_general | solution.py:52
  (6 shorter events, 0.1 us)
Async XLA Ops:
  6.5 175.7 %all-reduce.4.cloned.1.call-start = ((), (), s32[]{:S(2)}) async-start(), calls=%async_computation | async-start | bytes 2097152 | tf_op jit(solution)/shard_map/psum | solution.py:11
  39.2 0.7 copy-start
Sparse Core Ops, SparseCore 0:
  106.6 75.5 all-reduce.3
where the time goes:
time: 193 us; the launch traced here: 192 us
  blocking collectives  79.6 us (41%)
  waiting for transfers between devices  75.8 us (39%)
  between operations  13.4 us (7%)
  loops' own time  9.75 us (5%)
  matrix products  6.01 us (3%)
  local copies, waits for them, and re-layouts  4.25 us (2%)
  other arithmetic  3.19 us (2%)
    psum x1, waiting for transfers between devices, spread(): return lax.psum(jnp.where(mine, value, jnp.zeros_like(value)), axis)  75.7 us
    psum x1, blocking collectives, body(): mu_half = lax.psum(partial_value, 'col').astype(jnp.bfloat16)  50 us
    all_gather x1, blocking collectives, body(): gathered = lax.all_gather(coeff, 'row', axis=0, tiled=True)  29.6 us
    another operation x1, loops' own time, body(): partial_value = lax.fori_loop(0, live_count, add_slot, partial_value)  9.75 us
  transfers between devices with their start and end apart: 1, of which 1 were waited for; matrix products, arithmetic and copies ran while one was open for 0% of the time, Pallas kernels for 0%

commit v1 on v0

--- a/solution.py
+++ b/solution.py
@@ -15,7 +15,12 @@
     block_size = three_index.shape[4]
     aux_count = three_index.shape[3]
     occ_count = coeff.shape[1]
-    gathered = lax.all_gather(coeff, "row", axis=0, tiled=True)
+    ring = [coeff]
+    for hop in range(7):
+        ring.append(lax.ppermute(ring[-1], "row", [(dev, (dev + 1) % 8) for dev in range(8)]))
+    gathered = jnp.roll(
+        jnp.concatenate(ring[::-1], axis=0), (lax.axis_index("row") + 1) * ring[0].shape[0], axis=0
+    )
     nu_blocks = gathered.shape[0] // block_size
     occ_blocks = occ_count // block_size
     keep = occ_mask.astype(jnp.bfloat16)[:, None, :, None]

time: 193 us -> 212 us (1.098)
  waiting for transfers between devices: 75.8 us -> 121 us
  blocking collectives: 79.6 us -> 50.4 us
  starting transfers between devices: 0.01 us -> 3.07 us
    ppermute x0 -> x7, waiting for transfers between devices: none -> 45.3 us  [body(): lax.ppermute(ring[-1], 'row', [(dev, (dev + 1) % 8) for dev in range(8)])]
    all_gather x1 -> x0, blocking collectives: 29.6 us -> none  [body(): gathered = lax.all_gather(coeff, 'row', axis=0, tiled=True)]
    ppermute x0 -> x7, starting transfers between devices: none -> 3.06 us  [body(): lax.ppermute(ring[-1], 'row', [(dev, (dev + 1) % 8) for dev in range(8)])]
  transfers between devices with their start and end apart: 1 -> 8, of which waited for: 1 -> 8; matrix products, arithmetic and copies ran while one was open for 0% -> 1% of each run, Pallas kernels for 0% -> 0%
where the time goes in v1:
time: 212 us
  waiting for transfers between devices  121 us (57%)
  blocking collectives  50.4 us (24%)
  between operations  13.5 us (6%)
  loops' own time  9.77 us (5%)
  matrix products  6.01 us (3%)
  local copies, waits for them, and re-layouts  4.42 us (2%)
  other arithmetic  3.31 us (2%)
  starting transfers between devices  3.07 us (1%)
    psum x1, waiting for transfers between devices, spread(): return lax.psum(jnp.where(mine, value, jnp.zeros_like(value)), axis)  75.6 us
    psum x1, blocking collectives, body(): mu_half = lax.psum(partial_value, 'col').astype(jnp.bfloat16)  50.4 us
    ppermute x7, waiting for transfers between devices, body(): lax.ppermute(ring[-1], 'row', [(dev, (dev + 1) % 8) for dev in range(8)])  45.3 us
    another operation x1, loops' own time, body(): partial_value = lax.fori_loop(0, live_count, add_slot, partial_value)  9.77 us
  transfers between devices with their start and end apart: 8, of which 8 were waited for; matrix products, arithmetic and copies ran while one was open for 1% of the time, Pallas kernels for 0%

profile of v1, /device:TPU:0, one launch (start us, length us, event | category | flops | bytes accessed | tf_op | source)
XLA Modules:
  0.0 211.5 jit_solution(941608245201623549)
XLA Ops:
  6.5 0.0 all-reduce.4.cloned.1.call-start
  6.5 0.9 copy.5
  7.5 3.0 %collective-permute-start = (bf16[128,256]{0,1:T(8,128)(2,1)S(1)}, bf16[128,256]{0,1:T(8,128)(2,1)S(1)}, u32[]{:S(2)}, u32[]{:S(2)}) collective-permute-start(bf16[128,256]{0,1:T(8,128)(2,1)S(1)} %copy.5), channel_id=1, source_target_pairs={{0,4},{4,8},{8,12},{12,16},{16,20},{20,24},{24,28},{28,0},{1,5},{5... | collective-permute-start | bytes 196616 | tf_op jit(solution)/shard_map/ppermute | solution.py:20
  10.5 5.3 %collective-permute-done = bf16[128,256]{0,1:T(8,128)(2,1)S(1)} collective-permute-done((bf16[128,256]{0,1:T(8,128)(2,1)S(1)}, bf16[128,256]{0,1:T(8,128)(2,1)S(1)}, u32[]{:S(2)}, u32[]{:S(2)}) %collective-permute-start) | collective-permute-done | bytes 65568 | tf_op jit(solution)/shard_map/ppermute | solution.py:20
  15.8 0.0 collective-permute-start.1
  15.8 7.0 %collective-permute-done.1 = bf16[128,256]{0,1:T(8,128)(2,1)S(1)} collective-permute-done((bf16[128,256]{0,1:T(8,128)(2,1)S(1)}, bf16[128,256]{0,1:T(8,128)(2,1)S(1)}, u32[]{:S(2)}, u32[]{:S(2)}) %collective-permute-start.1) | collective-permute-done | bytes 65568 | tf_op jit(solution)/shard_map/ppermute | solution.py:20
  22.8 0.0 collective-permute-start.2
  22.8 7.0 %collective-permute-done.2 = bf16[128,256]{0,1:T(8,128)(2,1)S(1)} collective-permute-done((bf16[128,256]{0,1:T(8,128)(2,1)S(1)}, bf16[128,256]{0,1:T(8,128)(2,1)S(1)}, u32[]{:S(2)}, u32[]{:S(2)}) %collective-permute-start.2) | collective-permute-done | bytes 65568 | tf_op jit(solution)/shard_map/ppermute | solution.py:20
  29.8 0.0 collective-permute-start.3
  29.8 7.0 %collective-permute-done.3 = bf16[128,256]{0,1:T(8,128)(2,1)S(1)} collective-permute-done((bf16[128,256]{0,1:T(8,128)(2,1)S(1)}, bf16[128,256]{0,1:T(8,128)(2,1)S(1)}, u32[]{:S(2)}, u32[]{:S(2)}) %collective-permute-start.3) | collective-permute-done | bytes 65568 | tf_op jit(solution)/shard_map/ppermute | solution.py:20
  36.7 0.0 collective-permute-start.4
  36.7 7.3 %collective-permute-done.4 = bf16[128,256]{0,1:T(8,128)(2,1)S(1)} collective-permute-done((bf16[128,256]{0,1:T(8,128)(2,1)S(1)}, bf16[128,256]{0,1:T(8,128)(2,1)S(1)}, u32[]{:S(2)}, u32[]{:S(2)}) %collective-permute-start.4) | collective-permute-done | bytes 65568 | tf_op jit(solution)/shard_map/ppermute | solution.py:20
  44.0 0.0 collective-permute-start.5
  44.0 0.7 convert_element_type.13
  44.7 6.3 %collective-permute-done.5 = bf16[128,256]{0,1:T(8,128)(2,1)S(1)} collective-permute-done((bf16[128,256]{0,1:T(8,128)(2,1)S(1)}, bf16[128,256]{0,1:T(8,128)(2,1)S(1)}, u32[]{:S(2)}, u32[]{:S(2)}) %collective-permute-start.5) | collective-permute-done | bytes 65568 | tf_op jit(solution)/shard_map/ppermute | solution.py:20
  51.0 0.0 collective-permute-start.6
  51.0 1.4 fusion.10
  52.4 5.6 %collective-permute-done.6 = bf16[128,256]{0,1:T(8,128)(2,1)S(1)} collective-permute-done((bf16[128,256]{0,1:T(8,128)(2,1)S(1)}, bf16[128,256]{0,1:T(8,128)(2,1)S(1)}, u32[]{:S(2)}, u32[]{:S(2)}) %collective-permute-start.6) | collective-permute-done | bytes 65568 | tf_op jit(solution)/shard_map/ppermute | solution.py:20
  58.3 0.1 mul.31
  58.5 0.0 copy-start
  58.5 0.2 bitcast_multiply_fusion.1
  58.7 0.1 broadcast_in_dim.4.clone
  58.8 0.4 copy-done
  59.1 15.5 %while.12 = (s32[]{:T(128)}, f32[512,2,256]{2,0,1:T(8,128)S(1)}, s32[]{:T(128)}, s32[8]{0:T(128)S(1)}, bf16[1024,256]{0,1:T(8,128)(2,1)S(1)}, /*index=5*/bf16[8,...) while((s32[]{:T(128)}, f32[512,2,256]{2,0,1:T(8,128)S(1)}, ...), condition=%wide.region_2.3_spmd, body=%wide.region_1.2_spmd.sunk | while | flops 16842784 | bytes 2752994 | solution.py:47
  59.8 0.6 dynamic_slice.46
  62.7 0.1 copy.16
  62.8 1.0 fusion.19
  63.9 0.1 copy.17
  64.8 0.6 dynamic_slice.46
  67.6 0.1 copy.16
  67.8 1.0 fusion.19
  68.8 0.1 copy.17
  69.7 0.6 dynamic_slice.46
  72.6 0.1 copy.16
  72.7 1.0 fusion.19
  73.8 0.1 copy.17
  74.6 50.4 %all-reduce.5 = bf16[512,2,256]{2,0,1:T(8,128)(2,1)S(1)} all-reduce(f32[512,2,256]{2,0,1:T(8,128)S(1)} %get-tuple-element.88), channel_id=1, replica_groups=mesh['row'=8,'col'=4] {'col'}, use_global_device_ids=true, to_apply=%region_3.4 | all-reduce | flops 262144 | bytes 1572864 | tf_op jit(solution)/shard_map/psum | solution.py:50
  125.0 1.1 broadcast_select_fusion.1
  126.1 0.0 all-reduce.4.cloned.1.call-update
  126.1 75.6 %all-reduce.4.cloned.1.call-done = (bf16[512,2,256]{2,0,1:T(8,128)(2,1)}, bf16[512,2,256]{2,0,1:T(8,128)(2,1)}) async-done(((bf16[512,2,256]{2,0,1:T(8,128)(2,1)}, bf16[512,2,256]{2,0,1:T(8,128)(2,1)}), (bf16[512,2,256]{2,0,1:T(8,128)(2,1)}, bf16[512,2,256]{2,0,1:T(8,128)(2,1)})) %all-reduce.4.cloned.1.call-update) | async-done | bytes 1048592 | tf_op jit(solution)/shard_map/psum | solution.py:11
  201.8 2.9 %fusion.6 = bf16[512,1024]{1,0:T(8,128)(2,1)} fusion(bf16[512,2,256]{2,0,1:T(8,128)(2,1)} %get-tuple-element.101, bf16[512,2,256]{2,0,1:T(8,128)(2,1)} %get-tuple-element.102, bf16[512,2,256]{2,0,1:T(8,128)(2,1)S(1)} %all-reduce.5), kind=kOutput, calls=%fused_computation.10 | convolution fusion | flops 540016640 | bytes 2621440 | tf_op jit(solution)/shard_map/dot_general | solution.py:57
  (22 shorter events, 0.5 us)
Async XLA Ops:
  6.5 195.2 %all-reduce.4.cloned.1.call-start = ((), (), s32[]{:S(2)}) async-start(), calls=%async_computation | async-start | bytes 2097152 | tf_op jit(solution)/shard_map/psum | solution.py:11
  7.5 8.3 %collective-permute-start = (bf16[128,256]{0,1:T(8,128)(2,1)S(1)}, bf16[128,256]{0,1:T(8,128)(2,1)S(1)}, u32[]{:S(2)}, u32[]{:S(2)}) collective-permute-start(bf16[128,256]{0,1:T(8,128)(2,1)S(1)} %copy.5), channel_id=1, source_target_pairs={{0,4},{4,8},{8,12},{12,16},{16,20},{20,24},{24,28},{28,0},{1,5},{5... | collective-permute-start | bytes 196616 | tf_op jit(solution)/shard_map/ppermute | solution.py:20
  15.8 7.0 %collective-permute-start.1 = (bf16[128,256]{0,1:T(8,128)(2,1)S(1)}, bf16[128,256]{0,1:T(8,128)(2,1)S(1)}, u32[]{:S(2)}, u32[]{:S(2)}) collective-permute-start(bf16[128,256]{0,1:T(8,128)(2,1)S(1)} %collective-permute-done), channel_id=1, source_target_pairs={{0,4},{4,8},{8,12},{12,16},{16,20},{20,24},{24,28},{28,0},{1,5},{5... | collective-permute-start | bytes 196616 | tf_op jit(solution)/shard_map/ppermute | solution.py:20
  22.8 7.0 %collective-permute-start.2 = (bf16[128,256]{0,1:T(8,128)(2,1)S(1)}, bf16[128,256]{0,1:T(8,128)(2,1)S(1)}, u32[]{:S(2)}, u32[]{:S(2)}) collective-permute-start(bf16[128,256]{0,1:T(8,128)(2,1)S(1)} %collective-permute-done.1), channel_id=1, source_target_pairs={{0,4},{4,8},{8,12},{12,16},{16,20},{20,24},{24,28},{28,0},{1,5},{5... | collective-permute-start | bytes 196616 | tf_op jit(solution)/shard_map/ppermute | solution.py:20
  29.8 7.0 %collective-permute-start.3 = (bf16[128,256]{0,1:T(8,128)(2,1)S(1)}, bf16[128,256]{0,1:T(8,128)(2,1)S(1)}, u32[]{:S(2)}, u32[]{:S(2)}) collective-permute-start(bf16[128,256]{0,1:T(8,128)(2,1)S(1)} %collective-permute-done.2), channel_id=1, source_target_pairs={{0,4},{4,8},{8,12},{12,16},{16,20},{20,24},{24,28},{28,0},{1,5},{5... | collective-permute-start | bytes 196616 | tf_op jit(solution)/shard_map/ppermute | solution.py:20
  36.7 7.3 %collective-permute-start.4 = (bf16[128,256]{0,1:T(8,128)(2,1)S(1)}, bf16[128,256]{0,1:T(8,128)(2,1)S(1)}, u32[]{:S(2)}, u32[]{:S(2)}) collective-permute-start(bf16[128,256]{0,1:T(8,128)(2,1)S(1)} %collective-permute-done.3), channel_id=1, source_target_pairs={{0,4},{4,8},{8,12},{12,16},{16,20},{20,24},{24,28},{28,0},{1,5},{5... | collective-permute-start | bytes 196616 | tf_op jit(solution)/shard_map/ppermute | solution.py:20
  44.0 7.0 %collective-permute-start.5 = (bf16[128,256]{0,1:T(8,128)(2,1)S(1)}, bf16[128,256]{0,1:T(8,128)(2,1)S(1)}, u32[]{:S(2)}, u32[]{:S(2)}) collective-permute-start(bf16[128,256]{0,1:T(8,128)(2,1)S(1)} %collective-permute-done.4), channel_id=1, source_target_pairs={{0,4},{4,8},{8,12},{12,16},{16,20},{20,24},{24,28},{28,0},{1,5},{5... | collective-permute-start | bytes 196616 | tf_op jit(solution)/shard_map/ppermute | solution.py:20
  51.0 7.0 %collective-permute-start.6 = (bf16[128,256]{0,1:T(8,128)(2,1)S(1)}, bf16[128,256]{0,1:T(8,128)(2,1)S(1)}, u32[]{:S(2)}, u32[]{:S(2)}) collective-permute-start(bf16[128,256]{0,1:T(8,128)(2,1)S(1)} %collective-permute-done.5), channel_id=1, source_target_pairs={{0,4},{4,8},{8,12},{12,16},{16,20},{20,24},{24,28},{28,0},{1,5},{5... | collective-permute-start | bytes 196616 | tf_op jit(solution)/shard_map/ppermute | solution.py:20
  58.5 0.7 copy-start
Sparse Core Ops, SparseCore 0:
  126.2 75.4 all-reduce.3

commit v2 on v0

--- a/solution.py
+++ b/solution.py
@@ -8,7 +8,7 @@
 
 def spread(value, axis, root):
     mine = lax.axis_index(axis) == root
-    return lax.psum(jnp.where(mine, value, jnp.zeros_like(value)), axis)
+    return jnp.sum(lax.all_gather(jnp.where(mine, value, jnp.zeros_like(value)), axis), axis=0)
 
 
 def body(three_index, slot_pair, coeff, occ_mask):

time: 193 us -> 262 us (1.36)
  waiting for transfers between devices: 75.8 us -> 141 us
  other arithmetic: 3.19 us -> 9.17 us
    all_gather x0 -> x2, waiting for transfers between devices: none -> 140 us  [spread(): lax.all_gather(jnp.where(mine, value, jnp.zeros_like(value)), axis)]
    psum x1 -> x0, waiting for transfers between devices: 75.7 us -> none  [spread(): return lax.psum(jnp.where(mine, value, jnp.zeros_like(value)), axis)]
    reduce_sum x0 -> x2, other arithmetic: none -> 5.88 us  [spread(): jnp.sum(lax.all_gather(jnp.where(mine, value, jnp.zeros_like(value)), axi...]
  transfers between devices with their start and end apart: 1 -> 2, of which waited for: 1 -> 2; matrix products, arithmetic and copies ran while one was open for 0% -> 1% of each run, Pallas kernels for 0% -> 0%
where the time goes in v2:
time: 262 us; the launch traced here: 261 us
  waiting for transfers between devices  141 us (54%)
  blocking collectives  79.6 us (30%)
  between operations  13.5 us (5%)
  loops' own time  9.75 us (4%)
  other arithmetic  9.17 us (4%)
  matrix products  4.81 us (2%)
  local copies, waits for them, and re-layouts  3.76 us (1%)
    all_gather x2, waiting for transfers between devices, spread(): lax.all_gather(jnp.where(mine, value, jnp.zeros_like(value)), axis)  140 us
    psum x1, blocking collectives, body(): mu_half = lax.psum(partial_value, 'col').astype(jnp.bfloat16)  50.1 us
    all_gather x1, blocking collectives, body(): gathered = lax.all_gather(coeff, 'row', axis=0, tiled=True)  29.6 us
    another operation x1, loops' own time, body(): partial_value = lax.fori_loop(0, live_count, add_slot, partial_value)  9.75 us
    reduce_sum x2, other arithmetic, spread(): jnp.sum(lax.all_gather(jnp.where(mine, value, jnp.zeros_like(value)), axi...  5.88 us
  transfers between devices with their start and end apart: 2, of which 2 were waited for; matrix products, arithmetic and copies ran while one was open for 1% of the time, Pallas kernels for 0%

profile of v2, /device:TPU:0, one launch (start us, length us, event | category | flops | bytes accessed | tf_op | source)
XLA Modules:
  0.0 261.3 jit_solution(12359686313882612836)
XLA Ops:
  6.5 0.0 copy-start
  6.5 0.0 all-gather.5.cloned.1.call-start
  6.5 1.4 fusion.10
  8.0 0.7 convert_element_type.17
  8.7 0.9 copy.5
  9.6 29.6 %all_gather.15 = bf16[1024,256]{0,1:T(8,128)(2,1)S(1)} all-gather(bf16[128,256]{0,1:T(8,128)(2,1)S(1)} %copy.5), channel_id=1, replica_groups=mesh['row'=8,'col'=4] {'row'}, dimensions={0}, use_global_device_ids=true | all-gather | bytes 589824 | tf_op jit(solution)/shard_map/all_gather | solution.py:18
  39.2 0.1 mul.27
  39.3 0.1 bitcast_multiply_fusion.1
  39.4 0.1 broadcast_in_dim.4.clone
  39.5 0.0 copy-done
  39.5 15.5 %while.12 = (s32[]{:T(128)}, f32[512,2,256]{2,0,1:T(8,128)S(1)}, s32[]{:T(128)}, s32[8]{0:T(128)S(1)}, bf16[1024,256]{0,1:T(8,128)(2,1)S(1)}, /*index=5*/bf16[8,...) while((s32[]{:T(128)}, f32[512,2,256]{2,0,1:T(8,128)S(1)}, ...), condition=%wide.region_2.3_spmd, body=%wide.region_1.2_spmd.sunk | while | flops 16842784 | bytes 2753002 | solution.py:42
  40.2 0.6 dynamic_slice.40
  43.1 0.1 copy.14
  43.2 1.0 fusion.19
  44.2 0.1 copy.15
  45.1 0.6 dynamic_slice.40
  48.0 0.1 copy.14
  48.1 1.0 fusion.19
  49.2 0.1 copy.15
  50.0 0.6 dynamic_slice.40
  52.9 0.1 copy.14
  53.0 1.0 fusion.19
  54.1 0.1 copy.15
  55.0 50.1 %all-reduce.1 = bf16[512,2,256]{2,0,1:T(8,128)(2,1)S(1)} all-reduce(f32[512,2,256]{2,0,1:T(8,128)S(1)} %get-tuple-element.88), channel_id=1, replica_groups=mesh['row'=8,'col'=4] {'col'}, use_global_device_ids=true, to_apply=%region_3.4 | all-reduce | flops 262144 | bytes 1572864 | tf_op jit(solution)/shard_map/psum | solution.py:45
  105.0 1.1 broadcast_select_fusion.1
  106.1 0.0 all-gather.5.cloned.1.call-update
  106.1 0.0 all-gather.7.cloned.1.call-start
  106.2 0.7 all-gather.7.cloned.1.call-update
  106.9 69.4 %all-gather.5.cloned.1.call-done = bf16[4096,2,256]{2,0,1:T(8,128)(2,1)} async-done(((bf16[512,2,256]{2,0,1:T(8,128)(2,1)}), bf16[4096,2,256]{2,0,1:T(8,128)(2,1)}) %all-gather.5.cloned.1.call-update) | async-done | bytes 4194320 | tf_op jit(solution)/shard_map/all_gather | solution.py:11
  176.3 2.9 %reduce_sum.34 = bf16[512,2,256]{2,0,1:T(8,128)(2,1)S(1)} reduce(bf16[8,512,2,256]{3,1,0,2:T(8,128)(2,1)} %bitcast.35, bf16[]{:T(256)} %constant.87.clone.1), dimensions={0}, to_apply=%region_4.5 | reduce | flops 1835008 | bytes 4718594 | tf_op jit(solution)/shard_map/reduce_sum | solution.py:11
  179.3 70.6 %all-gather.7.cloned.1.call-done = bf16[4096,2,256]{2,0,1:T(8,128)(2,1)} async-done(((bf16[512,2,256]{2,0,1:T(8,128)(2,1)}), bf16[4096,2,256]{2,0,1:T(8,128)(2,1)}) %all-gather.7.cloned.1.call-update) | async-done | bytes 4194320 | tf_op jit(solution)/shard_map/all_gather | solution.py:11
  249.8 2.9 %reduce_sum.35 = bf16[512,2,256]{2,0,1:T(8,128)(2,1)S(1)} reduce(bf16[8,512,2,256]{3,1,0,2:T(8,128)(2,1)} %bitcast.36, bf16[]{:T(256)} %constant.87.clone.1), dimensions={0}, to_apply=%region_5.6 | reduce | flops 1835008 | bytes 4718594 | tf_op jit(solution)/shard_map/reduce_sum | solution.py:11
  252.8 1.7 fusion.6
  (6 shorter events, 0.1 us)
Async XLA Ops:
  6.5 32.9 %copy-start = (s32[1,1,8]{2,1,0:T(1,128)S(1)}, s32[1,1,8]{2,1,0:T(1,128)}, u32[]{:S(2)}) copy-start(s32[1,1,8]{2,1,0:T(1,128)} %param.7) | copy-start | bytes 100
  6.5 169.8 %all-gather.5.cloned.1.call-start = ((), (), s32[]{:S(2)}) async-start(), calls=%async_computation | async-start | bytes 4718592 | tf_op jit(solution)/shard_map/all_gather | solution.py:11
  106.1 143.7 %all-gather.7.cloned.1.call-start = ((), (), s32[]{:S(2)}) async-start(), calls=%async_computation.1 | async-start | bytes 4718592 | tf_op jit(solution)/shard_map/all_gather | solution.py:11
Sparse Core Ops, SparseCore 0:
  106.3 70.0 all-gather.4
  178.5 71.2 all-gather.6
